TPU v7x, 128 devices: a whole 4x4x4 slice. The times are simulated.
128 devices in a mesh: dp: 8 (over z, y_hi), head: 16 (over y_lo, x, core).
Axes of the slice: x: 4, y: 4 (y_hi: 2, y_lo: 2; y = y_hi * 2 + y_lo), z: 4, core: 2. Of those that a mesh axis runs over, the one named last changes fastest.
Arguments:
- ckpt_query: bfloat16 [4, 8192, 8192], P(None, ('dp', 'head')), may hold values from -0.125 to 0.125
- ckpt_key: bfloat16 [4, 8192, 1024], P(None, ('dp', 'head')), may hold values from -0.125 to 0.125
- ckpt_value: bfloat16 [4, 8192, 1024], P(None, ('dp', 'head')), may hold values from -0.125 to 0.125
- ckpt_output: bfloat16 [4, 8192, 8192], P(None, ('head', 'dp')), may hold values from -0.125 to 0.125
- hidden_in: bfloat16 [4096, 8192], P('dp'), may hold values from -17 to 17
- segment_ids: int32 [8, 512], P('dp'), may hold values from 0 to 3, never falling along the last dimension, each value on 1 to 256 neighbouring positions
Outputs:
- attn_out: bfloat16 [4096, 8192], P('dp', 'head')
All inputs are finite; a program needn't handle non-finite values.
Results may differ from a plain program's by a relative error of at most 0.01.
The roundings to bfloat16 on the way count: a program that leaves them out, or rounds other values in their place, can miss the bound.
Values may be sent and summed in bfloat16 or wider, within the bound.
A program may use at most 128 MiB of HBM per device.

v0:
```python
import jax
import jax.numpy as jnp
from jax import lax
from jax.sharding import PartitionSpec as P

rope_base = 500000.0


def from_partner(value, axis, apart):
    mask = 2**apart
    pairs = [(source, source ^ mask) for source in range(lax.axis_size(axis))]
    return lax.ppermute(value, axis, pairs)


def average(stack):
    return (jnp.sum(stack.astype(jnp.float32), axis=0) * 0.25).astype(jnp.bfloat16)


def rotate(values, positions):
    half = values.shape[-1] // 2
    freq = rope_base ** (-2.0 * jnp.arange(half, dtype=jnp.float32) / values.shape[-1])
    angle = positions[:, None] * freq[None, :]
    cosine = jnp.cos(angle)[:, None, :]
    sine = jnp.sin(angle)[:, None, :]
    first = values[..., :half]
    second = values[..., half:]
    return jnp.concatenate(
        [first * cosine - second * sine, second * cosine + first * sine], axis=-1
    )


def shards(ckpt_query, ckpt_key, ckpt_value, ckpt_output, hidden_in, segment_ids):
    output_weight = None
    moved = (
        lax.all_to_all(ckpt_query, "head", split_axis=2, concat_axis=1, tiled=True),
        lax.all_to_all(ckpt_key, "head", split_axis=2, concat_axis=1, tiled=True),
        lax.all_to_all(ckpt_value, "head", split_axis=2, concat_axis=1, tiled=True),
        lax.all_to_all(ckpt_output, "head", split_axis=2, concat_axis=1, tiled=True),
    )
    output_weight = average(moved[3])
    query_weight = average(moved[0])
    key_weight = average(moved[1])
    value_weight = average(moved[2])
    position = lax.axis_index("head")
    other_key, other_value = from_partner((key_weight, value_weight), "head", 0)
    lower = position // (1 << 0) % 2 == 0
    key_weight = jnp.where(
        lower,
        jnp.concatenate([key_weight, other_key], 1),
        jnp.concatenate([other_key, key_weight], 1),
    )
    value_weight = jnp.where(
        lower,
        jnp.concatenate([value_weight, other_value], 1),
        jnp.concatenate([other_value, value_weight], 1),
    )
    tok = hidden_in.shape[0]
    pieces = (
        lax.all_gather(query_weight, "dp", axis=0, tiled=True),
        lax.all_gather(key_weight, "dp", axis=0, tiled=True),
        lax.all_gather(value_weight, "dp", axis=0, tiled=True),
    )
    query, keys, values = tuple(
        (jnp.dot(hidden_in, piece, preferred_element_type=jnp.float32) for piece in pieces)
    )
    head_size = key_weight.shape[1]
    heads_here = query.shape[1] // head_size
    positions = jnp.arange(tok, dtype=jnp.float32)
    q_rot = rotate(query.reshape(tok, heads_here, head_size), positions).astype(jnp.bfloat16)
    k_rot = rotate(keys.reshape(tok, 1, head_size), positions)[:, 0].astype(jnp.bfloat16)
    v_b = values.astype(jnp.bfloat16)
    scores = jnp.einsum(
        "qhd,kd->hqk", q_rot, k_rot, preferred_element_type=jnp.float32
    ) * head_size ** (-0.5)
    order = jnp.arange(tok, dtype=jnp.int32)
    segment = segment_ids[0]
    allowed = (order[:, None] >= order[None, :]) & (segment[:, None] == segment[None, :])
    scores = jnp.where(allowed[None], scores, -1e30)
    peak = jnp.max(scores, axis=-1, keepdims=True)
    weights = jnp.exp(scores - peak)
    probs = (weights / jnp.sum(weights, axis=-1, keepdims=True)).astype(jnp.bfloat16)
    context = jnp.einsum("hqk,kd->qhd", probs, v_b, preferred_element_type=jnp.float32)
    context = context.astype(jnp.bfloat16).reshape(tok, heads_here * head_size)
    full = lax.dot_general(
        context,
        lax.all_gather(output_weight, "dp", axis=0, tiled=True),
        (((1,), (1,)), ((), ())),
        preferred_element_type=jnp.float32,
    )
    n_dp = lax.axis_size("dp")
    n_head = lax.axis_size("head")
    shard_rows = full.shape[1] // (n_dp * n_head)
    shaped = full.reshape(tok, n_dp, n_head, shard_rows)
    mine = lax.psum_scatter(shaped, "head", scatter_dimension=2, tiled=True)
    return mine.reshape(tok, n_dp * shard_rows).astype(jnp.bfloat16)


def solution(mesh):
    placed = (
        P(None, ("dp", "head"), None),
        P(None, ("dp", "head"), None),
        P(None, ("dp", "head"), None),
        P(None, ("head", "dp"), None),
        P("dp", None),
        P("dp", None),
    )
    return jax.shard_map(
        shards, mesh=mesh, in_specs=placed, out_specs=P("dp", "head"), check_vma=False
    )
```

profile of v0, /device:TPU:0, one launch (start us, length us, event | category | flops | bytes accessed | tf_op | source)
XLA Modules:
  0.0 680.2 jit_solution(2034700656391935076)
XLA Ops:
  6.5 1.6 copy.64
  8.1 1.5 reshape.173
  9.7 5.5 all-to-all-start.1
  15.2 12.7 %copy.67 = bf16[4,64,8192]{1,0,2:T(4,128)(2,1)} copy(bf16[4,64,8192]{2,1,0:T(8,128)(2,1)} %param.6) | data formatting | bytes 8388608 | tf_op args[0]
  27.9 14.0 %reshape.171 = bf16[16,2,65536]{2,1,0:T(2,128)(2,1)} reshape(bf16[8192,4,64]{2,1,0:T(4,128)(2,1)} %bitcast.80) | data formatting | bytes 8388608
  41.9 5.8 all-to-all-start.2
  47.7 0.7 reshape.174
  48.3 1.5 convert_reduce_fusion.2
  50.8 0.4 collective-permute-start.1
  51.2 1.0 collective-permute-done.1
  52.2 0.8 maximum_select_fusion.1
  53.0 0.5 all-gather.9.cloned.1.call-start
  53.5 50.5 %all-to-all-done.2 = bf16[16,2,65536]{2,1,0:T(2,128)(2,1)} async-done(((bf16[16,2,65536]{2,1,0:T(2,128)(2,1)}), bf16[16,2,65536]{2,1,0:T(2,128)(2,1)}, u32[]{:S(2)}, u32[]{:S(2)}) %all-to-all-start.2) | async-done | bytes 4194336 | tf_op jit(solution)/shard_map/all_to_all | solution.py:35
  104.0 13.7 %reshape.172 = bf16[8192,4,64]{2,1,0:T(4,128)(2,1)} reshape(bf16[16,2,65536]{2,1,0:T(2,128)(2,1)} %all-to-all-done.2) | data formatting | bytes 8388608
  117.7 33.7 %convert_reduce_fusion.1 = f32[64,8192]{0,1:T(8,128)} fusion(bf16[8192,4,64]{2,1,0:T(4,128)(2,1)} %reshape.172), kind=kLoop, calls=%fused_computation.2 | loop fusion | flops 3670016 | bytes 6291456 | tf_op jit(solution)/shard_map/reduce_sum | solution.py:16
  151.4 2.8 copy.68
  154.7 1.6 copy.69
  156.4 0.7 copy.61
  157.1 1.5 reshape.175
  158.6 4.6 all-to-all-start
  163.2 12.9 %copy.74 = bf16[4,64,8192]{1,0,2:T(4,128)(2,1)} copy(bf16[4,64,8192]{2,1,0:T(8,128)(2,1)} %param.9) | data formatting | bytes 8388608 | tf_op args[3]
  176.1 14.0 %reshape.177 = bf16[16,2,65536]{2,1,0:T(2,128)(2,1)} reshape(bf16[8192,4,64]{2,1,0:T(4,128)(2,1)} %bitcast.81) | data formatting | bytes 8388608
  190.2 5.8 all-to-all-start.3
  196.0 0.7 reshape.176
  196.6 1.5 convert_reduce_fusion.3
  198.5 0.4 copy.63
  199.1 0.4 collective-permute-start
  199.5 1.0 collective-permute-done
  200.5 0.8 maximum_select_fusion
  201.5 50.7 %all-to-all-done.3 = bf16[16,2,65536]{2,1,0:T(2,128)(2,1)} async-done(((bf16[16,2,65536]{2,1,0:T(2,128)(2,1)}), bf16[16,2,65536]{2,1,0:T(2,128)(2,1)}, u32[]{:S(2)}, u32[]{:S(2)}) %all-to-all-start.3) | async-done | bytes 4194336 | tf_op jit(solution)/shard_map/all_to_all | solution.py:38
  252.3 13.7 %reshape.178 = bf16[8192,4,64]{2,1,0:T(4,128)(2,1)} reshape(bf16[16,2,65536]{2,1,0:T(2,128)(2,1)} %all-to-all-done.3) | data formatting | bytes 8388608
  265.9 33.7 %convert_reduce_fusion = f32[64,8192]{0,1:T(8,128)} fusion(bf16[8192,4,64]{2,1,0:T(4,128)(2,1)} %reshape.178), kind=kLoop, calls=%fused_computation.1 | loop fusion | flops 3670016 | bytes 6291456 | tf_op jit(solution)/shard_map/reduce_sum | solution.py:16
  299.6 2.8 copy.75
  303.0 1.6 copy.76
  304.6 0.6 dynamic-slice
  305.5 1.0 fusion.14
  306.5 6.9 %convolution_bitcast_fusion = f32[512,1,128]{0,2,1:T(8,128)S(1)} fusion(bf16[8192,128]{0,1:T(8,128)(2,1)} %all-gather.7.cloned.1.call-done, bf16[512,8192]{1,0:T(8,128)(2,1)} %param.10), kind=kOutput, calls=%fused_computation.16 | convolution fusion | flops 1073741824 | bytes 10747904 | tf_op jit(solution)/shard_map/dot_general | solution.py:64
  313.4 0.6 subtract_convert_fusion.1
  314.0 10.0 %fusion.24 = f32[512,512]{1,0:T(8,128)S(1)} fusion(bf16[8192,512]{1,0:T(8,128)(2,1)} %all-gather.9.cloned.1.call-done, bf16[512,8192]{1,0:T(8,128)(2,1)} %param.10), kind=kOutput, calls=%fused_computation.49 | convolution fusion | flops 4294967296 | bytes 17825792 | tf_op jit(solution)/shard_map/dot_general | solution.py:64
  325.1 0.8 fusion.9
  325.9 4.0 fusion.23
  329.9 31.9 %all-gather.5.cloned.1.call-done = bf16[8192,128]{0,1:T(8,128)(2,1)} async-done(((bf16[1024,128]{0,1:T(8,128)(2,1)}), bf16[8192,128]{0,1:T(8,128)(2,1)}) %all-gather.5.cloned.1.call-update) | async-done | bytes 2097168 | tf_op jit(solution)/shard_map/all_gather | solution.py:61
  361.8 8.5 %fusion.6 = bf16[128,4,512]{2,0,1:T(8,128)(2,1)S(1)} fusion(f32[4,512,512]{1,2,0:T(8,128)} %get-tuple-element.14, f32[4,512]{1,0:T(4,128)S(1)} %get-tuple-element.13, bf16[8192,128]{0,1:T(8,128)(2,1)} %all-gather.5.cloned.1.call-done, bf16[512,8192]{1,0:T(8,128)(2,1)} %param.10), kind=kOutput, calls=%fused_computation.15 | convolution fusion | flops 1344602112 | bytes 15212544 | tf_op jit(solution)/shard_map/hqk,kd->qhd/dot_general | solution.py:82
  370.3 98.7 %all-gather.11.cloned.1.call-done = bf16[8192,512]{1,0:T(8,128)(2,1)} async-done(((bf16[1024,512]{1,0:T(8,128)(2,1)}), bf16[8192,512]{1,0:T(8,128)(2,1)}) %all-gather.11.cloned.1.call-update) | async-done | bytes 8388624 | tf_op jit(solution)/shard_map/all_gather | solution.py:86
  469.0 11.6 %fusion.25 = f32[512,8,16,64]{0,3,2,1:T(8,128)} fusion(bf16[512,512,1,1]{0,1,3,2:T(8,128)(2,1)S(1)} %bitcast.96, bf16[8,16,64,512]{3,2,1,0:T(8,128)(2,1)} %bitcast.95), kind=kOutput, calls=%fused_computation.50 | convolution fusion | flops 4294967296 | bytes 25690112 | tf_op jit(solution)/shard_map/dot_general | solution.py:84
  480.6 190.1 %all-reduce.2 = bf16[512,8,16,64]{0,3,2,1:T(8,128)(2,1)} all-reduce(f32[512,8,16,64]{0,3,2,1:T(8,128)} %fusion.25), channel_id=2, replica_groups=mesh['dp'=8,'head'=16] {'head'}, use_global_device_ids=true, to_apply=%region_6.7.clone | all-reduce | flops 4194304 | bytes 25165824
  670.7 1.7 dynamic-slice_convert_fusion
  672.4 1.0 copy.78
  (36 shorter events, 4.2 us)
Async XLA Ops:
  9.7 32.2 %all-to-all-start.1 = ((bf16[16,2,8192]{2,1,0:T(2,128)(2,1)}), bf16[16,2,8192]{2,1,0:T(2,128)(2,1)S(1)}, u32[]{:S(2)}, u32[]{:S(2)}) async-start(bf16[16,2,8192]{2,1,0:T(2,128)(2,1)} %reshape.173), calls=%async_computation.1 | async-start | bytes 1048576 | tf_op jit(solution)/shard_map/all_to_all | solution.py:36
  41.9 62.1 %all-to-all-start.2 = ((bf16[16,2,65536]{2,1,0:T(2,128)(2,1)}), bf16[16,2,65536]{2,1,0:T(2,128)(2,1)}, u32[]{:S(2)}, u32[]{:S(2)}) async-start(bf16[16,2,65536]{2,1,0:T(2,128)(2,1)} %reshape.171), calls=%async_computation.2 | async-start | bytes 8388608 | tf_op jit(solution)/shard_map/all_to_all | solution.py:35
  47.6 258.9 %all-gather.7.cloned.1.call-start = ((), (), s32[]{:S(2)}) async-start(), calls=%async_computation.5 | async-start | bytes 2359296 | tf_op jit(solution)/shard_map/all_gather | solution.py:60
  50.8 1.4 collective-permute-start.1
  53.0 261.0 %all-gather.9.cloned.1.call-start = ((), (), s32[]{:S(2)}) async-start(), calls=%async_computation.6 | async-start | bytes 9437184 | tf_op jit(solution)/shard_map/all_gather | solution.py:59
  154.2 2.1 copy-start
  158.6 31.5 %all-to-all-start = ((bf16[16,2,8192]{2,1,0:T(2,128)(2,1)}), bf16[16,2,8192]{2,1,0:T(2,128)(2,1)S(1)}, u32[]{:S(2)}, u32[]{:S(2)}) async-start(bf16[16,2,8192]{2,1,0:T(2,128)(2,1)} %reshape.175), calls=%async_computation | async-start | bytes 1048576 | tf_op jit(solution)/shard_map/all_to_all | solution.py:37
  190.2 62.1 %all-to-all-start.3 = ((bf16[16,2,65536]{2,1,0:T(2,128)(2,1)}), bf16[16,2,65536]{2,1,0:T(2,128)(2,1)}, u32[]{:S(2)}, u32[]{:S(2)}) async-start(bf16[16,2,65536]{2,1,0:T(2,128)(2,1)} %reshape.177), calls=%async_computation.3 | async-start | bytes 8388608 | tf_op jit(solution)/shard_map/all_to_all | solution.py:38
  195.9 165.9 %all-gather.5.cloned.1.call-start = ((), (), s32[]{:S(2)}) async-start(), calls=%async_computation.4 | async-start | bytes 2359296 | tf_op jit(solution)/shard_map/all_gather | solution.py:61
  199.1 1.4 collective-permute-start
  201.3 267.7 %all-gather.11.cloned.1.call-start = ((), (), s32[]{:S(2)}) async-start(), calls=%async_computation.7 | async-start | bytes 9437184 | tf_op jit(solution)/shard_map/all_gather | solution.py:86
  302.5 2.2 copy-start.2
  302.5 2.8 copy-start.1
Sparse Core Ops, SparseCore 0:
  53.1 73.8 all-gather.6
  156.5 150.6 all-gather.8
  309.5 52.2 all-gather.4
  364.0 104.9 all-gather.10
where the time goes:
time: 687 us; the launch traced here: 680 us
  waiting for transfers between devices  234 us (34%)
  blocking collectives  190 us (28%)
  local copies, waits for them, and re-layouts  103 us (15%)
  other arithmetic  78.1 us (11%)
  matrix products  37.9 us (6%)
  starting transfers between devices  23.3 us (3%)
  between operations  13.7 us (2%)
    unnamed x1, blocking collectives  190 us
    all_gather x1, waiting for transfers between devices, shards(): lax.all_gather(output_weight, 'dp', axis=0, tiled=True)  98.7 us
    unnamed x23, local copies, waits for them, and re-layouts  89.6 us
    reduce_sum x4, other arithmetic, average(): jnp.sum(stack.astype(jnp.float32), axis=0) * 0.25  70.3 us
    all_to_all x1, waiting for transfers between devices, shards(): lax.all_to_all(ckpt_output, 'head', split_axis=2, concat_axis=1, tiled=True)  50.7 us
    all_to_all x1, waiting for transfers between devices, shards(): lax.all_to_all(ckpt_query, 'head', split_axis=2, concat_axis=1, tiled=True)  50.5 us
    all_gather x1, waiting for transfers between devices, shards(): lax.all_gather(value_weight, 'dp', axis=0, tiled=True)  31.9 us
    dot_general x2, matrix products, shards(): jnp.dot(hidden_in, piece, preferred_element_type=jnp.float32)  17 us
  transfers between devices with their start and end apart: 10, of which 6 were waited for; matrix products, arithmetic and copies ran while one was open for 30% of the time, Pallas kernels for 0%

commit v1 on v0

--- a/solution.py
+++ b/solution.py
@@ -58,7 +58,9 @@
     pieces = (
         lax.all_gather(query_weight, "dp", axis=0, tiled=True),
         lax.all_gather(key_weight, "dp", axis=0, tiled=True),
-        lax.all_gather(value_weight, "dp", axis=0, tiled=True),
+        jnp.concatenate(
+            lax.all_to_all(jnp.stack([value_weight] * lax.axis_size("dp")), "dp", 0, 0), axis=0
+        ),
     )
     query, keys, values = tuple(
         (jnp.dot(hidden_in, piece, preferred_element_type=jnp.float32) for piece in pieces)

time: 687 us -> 652 us (0.949)
  waiting for transfers between devices: 234 us -> 131 us
  blocking collectives: 190 us -> 249 us
    all_to_all x0 -> x1, blocking collectives: none -> 59.2 us  [shards(): lax.all_to_all(ckpt_output, 'head', split_axis=2, concat_axis=1, tiled=True)]
    all_to_all x1, waiting for transfers between devices: 50.7 us -> 9.36 us  [shards(): lax.all_to_all(jnp.stack([value_weight] * lax.axis_size('dp')), 'dp', 0, 0)]
    all_gather x1, waiting for transfers between devices: 98.7 us -> 58.8 us  [shards(): lax.all_gather(output_weight, 'dp', axis=0, tiled=True)]
    all_gather x1 -> x0, waiting for transfers between devices: 31.9 us -> none  [shards(): lax.all_gather(value_weight, 'dp', axis=0, tiled=True)]
    all_to_all x1, waiting for transfers between devices: 0.01 us -> 9.24 us  [shards(): lax.all_to_all(ckpt_value, 'head', split_axis=2, concat_axis=1, tiled=True)]
  transfers between devices with their start and end apart: 10 -> 9, of which waited for: 6 -> 6; matrix products, arithmetic and copies ran while one was open for 30% -> 32% of each run, Pallas kernels for 0% -> 0%
where the time goes in v1:
time: 652 us; the launch traced here: 641 us
  blocking collectives  249 us (38%)
  waiting for transfers between devices  131 us (20%)
  local copies, waits for them, and re-layouts  105 us (16%)
  other arithmetic  77.4 us (12%)
  matrix products  38.4 us (6%)
  starting transfers between devices  26.7 us (4%)
  between operations  13.7 us (2%)
    unnamed x1, blocking collectives  190 us
    unnamed x23, local copies, waits for them, and re-layouts  89.6 us
    reduce_sum x4, other arithmetic, average(): jnp.sum(stack.astype(jnp.float32), axis=0) * 0.25  70.3 us
    all_to_all x1, blocking collectives, shards(): lax.all_to_all(ckpt_output, 'head', split_axis=2, concat_axis=1, tiled=True)  59.2 us
    all_gather x1, waiting for transfers between devices, shards(): lax.all_gather(output_weight, 'dp', axis=0, tiled=True)  58.8 us
    all_to_all x1, waiting for transfers between devices, shards(): lax.all_to_all(ckpt_query, 'head', split_axis=2, concat_axis=1, tiled=True)  50.9 us
    dot_general x2, matrix products, shards(): jnp.dot(hidden_in, piece, preferred_element_type=jnp.float32)  16.5 us
  transfers between devices with their start and end apart: 9, of which 6 were waited for; matrix products, arithmetic and copies ran while one was open for 32% of the time, Pallas kernels for 0%

profile of v1, /device:TPU:0, one launch (start us, length us, event | category | flops | bytes accessed | tf_op | source)
XLA Modules:
  0.0 640.8 jit_solution(10896600865397534193)
XLA Ops:
  6.5 1.6 copy.68
  8.1 1.5 reshape.190
  9.7 5.5 all-to-all-start.2
  15.2 12.7 %copy.71 = bf16[4,64,8192]{1,0,2:T(4,128)(2,1)} copy(bf16[4,64,8192]{2,1,0:T(8,128)(2,1)} %param.6) | data formatting | bytes 8388608 | tf_op args[0]
  27.9 14.0 %reshape.188 = bf16[16,2,65536]{2,1,0:T(2,128)(2,1)} reshape(bf16[8192,4,64]{2,1,0:T(4,128)(2,1)} %bitcast.81) | data formatting | bytes 8388608
  41.9 5.8 all-to-all-start.3
  47.7 0.7 reshape.191
  48.4 1.5 convert_reduce_fusion.2
  50.2 0.4 copy.70
  50.8 0.4 collective-permute-start.1
  51.3 1.0 collective-permute-done.1
  52.3 0.8 maximum_select_fusion.1
  53.1 50.9 %all-to-all-done.3 = bf16[16,2,65536]{2,1,0:T(2,128)(2,1)} async-done(((bf16[16,2,65536]{2,1,0:T(2,128)(2,1)}), bf16[16,2,65536]{2,1,0:T(2,128)(2,1)}, u32[]{:S(2)}, u32[]{:S(2)}) %all-to-all-start.3) | async-done | bytes 4194336 | tf_op jit(solution)/shard_map/all_to_all | solution.py:35
  104.0 13.7 %reshape.189 = bf16[8192,4,64]{2,1,0:T(4,128)(2,1)} reshape(bf16[16,2,65536]{2,1,0:T(2,128)(2,1)} %all-to-all-done.3) | data formatting | bytes 8388608
  117.7 33.7 %convert_reduce_fusion.1 = f32[64,8192]{0,1:T(8,128)} fusion(bf16[8192,4,64]{2,1,0:T(4,128)(2,1)} %reshape.189), kind=kLoop, calls=%fused_computation.2 | loop fusion | flops 3670016 | bytes 6291456 | tf_op jit(solution)/shard_map/reduce_sum | solution.py:16
  151.4 2.8 copy.72
  154.7 1.5 copy.73
  156.3 0.5 all-gather.8.cloned.1.call-start
  156.8 12.8 %copy.78 = bf16[4,64,8192]{1,0,2:T(4,128)(2,1)} copy(bf16[4,64,8192]{2,1,0:T(8,128)(2,1)} %param.9) | data formatting | bytes 8388608 | tf_op args[3]
  169.6 14.1 %reshape.194 = bf16[16,2,65536]{2,1,0:T(2,128)(2,1)} reshape(bf16[8192,4,64]{2,1,0:T(4,128)(2,1)} %bitcast.82) | data formatting | bytes 8388608
  183.7 59.2 %all_to_all.20 = bf16[16,2,65536]{2,1,0:T(2,128)(2,1)} all-to-all(bf16[16,2,65536]{2,1,0:T(2,128)(2,1)} %reshape.194), channel_id=1, replica_groups=mesh['dp'=8,'head'=16] {'head'}, dimensions={0} | all-to-all | bytes 8388608 | tf_op jit(solution)/shard_map/all_to_all | solution.py:38
  242.9 13.7 %reshape.195 = bf16[8192,4,64]{2,1,0:T(4,128)(2,1)} reshape(bf16[16,2,65536]{2,1,0:T(2,128)(2,1)} %all_to_all.20) | data formatting | bytes 8388608
  256.6 33.7 %convert_reduce_fusion = f32[64,8192]{0,1:T(8,128)} fusion(bf16[8192,4,64]{2,1,0:T(4,128)(2,1)} %reshape.195), kind=kLoop, calls=%fused_computation.1 | loop fusion | flops 3670016 | bytes 6291456 | tf_op jit(solution)/shard_map/reduce_sum | solution.py:16
  290.2 2.8 copy.79
  293.6 1.6 copy.80
  295.2 0.7 copy.64
  296.0 1.5 reshape.192
  297.5 6.0 all-to-all-start
  303.5 0.6 dynamic-slice
  304.2 1.0 fusion.14
  305.1 9.2 %all-to-all-done = bf16[16,2,8192]{2,1,0:T(2,128)(2,1)S(1)} async-done(((bf16[16,2,8192]{2,1,0:T(2,128)(2,1)}), bf16[16,2,8192]{2,1,0:T(2,128)(2,1)S(1)}, u32[]{:S(2)}, u32[]{:S(2)}) %all-to-all-start) | async-done | bytes 524320 | tf_op jit(solution)/shard_map/all_to_all | solution.py:37
  314.4 0.7 reshape.193
  315.0 1.5 convert_reduce_fusion.3
  317.8 1.1 collective-permute-done
  319.2 1.6 stack.2
  320.8 8.3 %all-to-all-start.1 = ((bf16[8,1024,128]{2,1,0:T(8,128)(2,1)}), bf16[8,1024,128]{2,1,0:T(8,128)(2,1)}, u32[]{:S(2)}, u32[]{:S(2)}) async-start(bf16[8,1024,128]{2,1,0:T(8,128)(2,1)} %stack.2), calls=%async_computation.1 | async-start | bytes 4194304 | tf_op jit(solution)/shard_map/all_to_all | solution.py:62
  329.1 7.0 %convolution_bitcast_fusion = f32[512,1,128]{0,2,1:T(8,128)S(1)} fusion(bf16[8192,128]{0,1:T(8,128)(2,1)} %all-gather.4.cloned.1.call-done, bf16[512,8192]{1,0:T(8,128)(2,1)} %param.10), kind=kOutput, calls=%fused_computation.16 | convolution fusion | flops 1073741824 | bytes 10747904 | tf_op jit(solution)/shard_map/dot_general | solution.py:66
  336.1 0.6 subtract_convert_fusion.1
  336.7 9.5 %fusion.24 = f32[512,512]{1,0:T(8,128)S(1)} fusion(bf16[8192,512]{1,0:T(8,128)(2,1)} %all-gather.6.cloned.1.call-done, bf16[512,8192]{1,0:T(8,128)(2,1)} %param.10), kind=kOutput, calls=%fused_computation.49 | convolution fusion | flops 4294967296 | bytes 17825792 | tf_op jit(solution)/shard_map/dot_general | solution.py:66
  347.3 0.8 fusion.9
  348.1 4.0 fusion.23
  352.0 9.4 %all-to-all-done.1 = bf16[8,1024,128]{2,1,0:T(8,128)(2,1)} async-done(((bf16[8,1024,128]{2,1,0:T(8,128)(2,1)}), bf16[8,1024,128]{2,1,0:T(8,128)(2,1)}, u32[]{:S(2)}, u32[]{:S(2)}) %all-to-all-start.1) | async-done | bytes 2097184 | tf_op jit(solution)/shard_map/all_to_all | solution.py:62
  361.4 9.2 %fusion.6 = bf16[128,4,512]{2,0,1:T(8,128)(2,1)S(1)} fusion(f32[4,512,512]{1,2,0:T(8,128)} %get-tuple-element.14, f32[4,512]{1,0:T(4,128)S(1)} %get-tuple-element.13, bf16[8192,128]{1,0:T(8,128)(2,1)} %bitcast.1, bf16[512,8192]{1,0:T(8,128)(2,1)} %param.10), kind=kOutput, calls=%fused_computation.15 | convolution fusion | flops 1344602112 | bytes 15212544 | tf_op jit(solution)/shard_map/hqk,kd->qhd/dot_general | solution.py:84
  370.6 58.8 %all-gather.8.cloned.1.call-done = bf16[8192,512]{1,0:T(8,128)(2,1)} async-done(((bf16[1024,512]{1,0:T(8,128)(2,1)}), bf16[8192,512]{1,0:T(8,128)(2,1)}) %all-gather.8.cloned.1.call-update) | async-done | bytes 8388624 | tf_op jit(solution)/shard_map/all_gather | solution.py:88
  429.4 11.8 %fusion.25 = f32[512,8,16,64]{0,3,2,1:T(8,128)} fusion(bf16[512,512,1,1]{0,1,3,2:T(8,128)(2,1)S(1)} %bitcast.97, bf16[8,16,64,512]{3,2,1,0:T(8,128)(2,1)} %bitcast.96), kind=kOutput, calls=%fused_computation.50 | convolution fusion | flops 4294967296 | bytes 25690112 | tf_op jit(solution)/shard_map/dot_general | solution.py:86
  441.3 190.1 %all-reduce.2 = bf16[512,8,16,64]{0,3,2,1:T(8,128)(2,1)} all-reduce(f32[512,8,16,64]{0,3,2,1:T(8,128)} %fusion.25), channel_id=2, replica_groups=mesh['dp'=8,'head'=16] {'head'}, use_global_device_ids=true, to_apply=%region_6.7.clone | all-reduce | flops 4194304 | bytes 25165824
  631.3 1.7 dynamic-slice_convert_fusion
  633.1 1.0 copy.82
  (36 shorter events, 4.2 us)
Async XLA Ops:
  9.7 32.2 %all-to-all-start.2 = ((bf16[16,2,8192]{2,1,0:T(2,128)(2,1)}), bf16[16,2,8192]{2,1,0:T(2,128)(2,1)S(1)}, u32[]{:S(2)}, u32[]{:S(2)}) async-start(bf16[16,2,8192]{2,1,0:T(2,128)(2,1)} %reshape.190), calls=%async_computation.2 | async-start | bytes 1048576 | tf_op jit(solution)/shard_map/all_to_all | solution.py:36
  41.9 62.1 %all-to-all-start.3 = ((bf16[16,2,65536]{2,1,0:T(2,128)(2,1)}), bf16[16,2,65536]{2,1,0:T(2,128)(2,1)}, u32[]{:S(2)}, u32[]{:S(2)}) async-start(bf16[16,2,65536]{2,1,0:T(2,128)(2,1)} %reshape.188), calls=%async_computation.3 | async-start | bytes 8388608 | tf_op jit(solution)/shard_map/all_to_all | solution.py:35
  47.7 281.4 %all-gather.4.cloned.1.call-start = ((), (), s32[]{:S(2)}) async-start(), calls=%async_computation.5 | async-start | bytes 2359296 | tf_op jit(solution)/shard_map/all_gather | solution.py:60
  50.8 1.4 collective-permute-start.1
  53.0 283.6 %all-gather.6.cloned.1.call-start = ((), (), s32[]{:S(2)}) async-start(), calls=%async_computation.6 | async-start | bytes 9437184 | tf_op jit(solution)/shard_map/all_gather | solution.py:59
  156.3 273.2 %all-gather.8.cloned.1.call-start = ((), (), s32[]{:S(2)}) async-start(), calls=%async_computation.7 | async-start | bytes 9437184 | tf_op jit(solution)/shard_map/all_gather | solution.py:88
  293.1 2.2 copy-start
  293.6 9.9 %copy-start.2 = (u32[128]{0:T(128)S(1)}, u32[128]{0:T(128)}, u32[]{:S(2)}) copy-start(u32[128]{0:T(128)} %constant.54) | copy-start | bytes 1540
  296.0 21.6 %copy-start.1 = (s32[1,512]{1,0:T(1,128)S(1)}, s32[1,512]{1,0:T(1,128)}, u32[]{:S(2)}) copy-start(s32[1,512]{1,0:T(1,128)} %param.11) | copy-start | bytes 6148
  297.5 16.9 %all-to-all-start = ((bf16[16,2,8192]{2,1,0:T(2,128)(2,1)}), bf16[16,2,8192]{2,1,0:T(2,128)(2,1)S(1)}, u32[]{:S(2)}, u32[]{:S(2)}) async-start(bf16[16,2,8192]{2,1,0:T(2,128)(2,1)} %reshape.192), calls=%async_computation | async-start | bytes 1048576 | tf_op jit(solution)/shard_map/all_to_all | solution.py:37
  317.5 1.4 collective-permute-start
  320.8 40.6 %all-to-all-start.1 = ((bf16[8,1024,128]{2,1,0:T(8,128)(2,1)}), bf16[8,1024,128]{2,1,0:T(8,128)(2,1)}, u32[]{:S(2)}, u32[]{:S(2)}) async-start(bf16[8,1024,128]{2,1,0:T(8,128)(2,1)} %stack.2), calls=%async_computation.1 | async-start | bytes 4194304 | tf_op jit(solution)/shard_map/all_to_all | solution.py:62
Sparse Core Ops, SparseCore 0:
  53.2 73.8 all-gather.3
  156.4 143.1 all-gather.5
  302.0 127.3 all-gather.7
